TPU v7x, 512 devices: a whole 4x4x16 slice. The times are simulated.
512 devices in a mesh: replica: 64 (over y, z_lo, core), tensor: 8 (over z_hi, x).
Axes of the slice: x: 4, y: 4, z: 16 (z_hi: 2, z_lo: 8; z = z_hi * 8 + z_lo), core: 2. Of those that a mesh axis runs over, the one named last changes fastest.
Arguments:
- hidden_act: bfloat16 [16384, 7168], P('replica', 'tensor'), may hold values from -15 to 15
- residual_in: bfloat16 [512, 65536], P('tensor', 'replica'), may hold values from -6 to 6
- cotangent: bfloat16 [512, 65536], P('tensor', 'replica'), may hold values from -6 to 6
- norm_gain: bfloat16 [2048], replicated, may hold values from 0.25 to 1.75
- inner_weight: bfloat16 [7168, 65536], P('tensor', 'replica'), may hold values from -24 to 24
- anchor: bfloat16 [7168, 2048], P('tensor', 'replica'), may hold values from -6 to 6
- momentum: bfloat16 [7168, 2048], P('tensor', 'replica'), may hold values from -3 to 3
Outputs:
- normed: bfloat16 [512, 65536], P('tensor', 'replica')
- mixed_weight: bfloat16 [7168, 65536], P('tensor', 'replica')
- momentum_out: bfloat16 [7168, 2048], P('tensor', 'replica')
All inputs are finite; a program needn't handle non-finite values.
Results may differ from a plain program's by a relative error of at most 0.0075.
Values may be sent and summed in bfloat16 or wider, within the bound.
A program may use at most 64 MiB of HBM per device.

v0:
```python
import math
import jax
import jax.numpy as jnp
from jax import lax
from jax.sharding import PartitionSpec as P

FF = 7168
TOK = 512
inner_rate = 0.2
outer_rate = 0.7
outer_mu = 0.9
mix_share = 0.5


def partner(array, axis, stride):
    return lax.ppermute(array, axis, [(i, i ^ 1 << stride) for i in range(lax.axis_size(axis))])


def norm_rows(out_rows, resid_rows, cot_rows, norm_scale, total_features):
    summed_in = resid_rows.astype(jnp.float32) + out_rows
    dz_rows = cot_rows.astype(jnp.float32) * norm_scale
    own_squares = jnp.sum(summed_in * summed_in, axis=-1)
    own_cross = jnp.sum(dz_rows * summed_in, axis=-1)
    other_squares, other_cross = partner((own_squares, own_cross), "replica", 0)
    mean_squares = ((own_squares + other_squares) / total_features)[:, None]
    inner_mean = ((own_cross + other_cross) / total_features)[:, None]
    root_inv = lax.rsqrt(mean_squares + 1e-05)
    normed = (summed_in * root_inv * norm_scale).astype(jnp.bfloat16)
    slopes = (root_inv * (dz_rows - summed_in * inner_mean * root_inv * root_inv)).astype(
        jnp.bfloat16
    )
    return (normed, slopes)


def local(hidden_act, residual_in, cotangent, norm_gain, inner_weight, anchor, momentum):
    ff_local = inner_weight.shape[0]
    half_cols = inner_weight.shape[1]
    total_features = 2 * half_cols
    multiplier = 1.0 / math.sqrt(FF)
    step_scale = inner_rate * math.sqrt(FF / TOK)
    side = lax.axis_index("replica") % 2
    first = side == 0
    norm_scale = lax.dynamic_slice_in_dim(norm_gain, side * half_cols, half_cols, 0).astype(
        jnp.float32
    )
    partner_rows = partner(hidden_act, "replica", 0)
    hidden_full = jnp.where(
        first,
        jnp.concatenate([hidden_act, partner_rows], 0),
        jnp.concatenate([partner_rows, hidden_act], 0),
    )
    contract = (((0,), (0,)), ((), ()))
    row_block = hidden_full
    out_rows = lax.psum_scatter(
        jnp.dot(row_block, inner_weight, preferred_element_type=jnp.float32) * multiplier,
        "tensor",
        scatter_dimension=0,
        tiled=True,
    )
    normed, slopes = norm_rows(out_rows, residual_in, cotangent, norm_scale, total_features)
    row_block = hidden_full
    gradient = lax.dot_general(
        row_block,
        lax.all_gather(slopes, "tensor", axis=0, tiled=True),
        contract,
        preferred_element_type=jnp.float32,
    )
    gradient = gradient * multiplier
    stepped = inner_weight.astype(jnp.float32) - step_scale * gradient
    replica_count = lax.axis_size("replica") // 2
    buffer = jnp.zeros((1, ff_local, total_features), jnp.bfloat16)
    buffer = lax.dynamic_update_slice(buffer, inner_weight[None], (0, 0, side * half_cols))
    received = lax.all_to_all(buffer, "replica", split_axis=2, concat_axis=0, tiled=True)
    summed = jnp.sum(received, axis=0, dtype=jnp.float32)
    anchor_f = anchor.astype(jnp.float32)
    pseudo = anchor_f - summed / replica_count
    moment = (outer_mu * momentum.astype(jnp.float32) + pseudo).astype(jnp.bfloat16)
    new_anchor = (anchor_f - outer_rate * (pseudo + outer_mu * moment.astype(jnp.float32))).astype(
        jnp.bfloat16
    )
    full_anchor = lax.all_gather(new_anchor, "replica", axis=1, tiled=True)
    own_anchor = lax.dynamic_slice_in_dim(full_anchor, side * half_cols, half_cols, 1)
    mixed = (mix_share * stepped + (1.0 - mix_share) * own_anchor.astype(jnp.float32)).astype(
        jnp.bfloat16
    )
    return (normed, mixed, moment)


def solution(mesh):
    in_specs = (
        P("replica", "tensor"),
        P("tensor", "replica"),
        P("tensor", "replica"),
        P(),
        P("tensor", "replica"),
        P("tensor", "replica"),
        P("tensor", "replica"),
    )
    out_specs = (P("tensor", "replica"), P("tensor", "replica"), P("tensor", "replica"))
    return jax.shard_map(local, mesh=mesh, in_specs=in_specs, out_specs=out_specs, check_vma=False)
```

profile of v0, /device:TPU:8, one launch (start us, length us, event | category | flops | bytes accessed | tf_op | source)
XLA Modules:
  0.0 599.8 jit_solution(8487567397777229452)
XLA Ops:
  8.0 9.8 %copy.20 = bf16[1,896,1024]{1,0,2:T(2,128)(2,1)} copy(bf16[1,896,1024]{2,1,0:T(8,128)(2,1)} %bitcast.9) | data formatting | bytes 3670016 | tf_op jit(solution)/shard_map/broadcast_in_dim | solution.py:72
  17.8 4.9 broadcast_in_dim.4
  22.7 5.6 constant_dynamic-update-slice_fusion
  28.3 0.5 broadcast.27
  28.8 79.9 %reduce.3 = bf16[2048,896]{1,0:T(8,128)(2,1)} reduce(bf16[2048,1,896]{2,1,0:T(2,128)(2,1)} %bitcast.3, bf16[]{:T(256)} %broadcast.27), dimensions={1}, to_apply=%bitcast.3.reduce_sub_computation | reduce | bytes 7340034
  108.7 8.3 %reshape.16 = bf16[64,2,14336]{2,1,0:T(2,128)(2,1)} reshape(bf16[2048,896]{1,0:T(8,128)(2,1)} %reduce.3) | data formatting | bytes 7340032
  117.0 16.5 %all-to-all-start = ((bf16[64,2,14336]{2,1,0:T(2,128)(2,1)}), bf16[64,2,14336]{2,1,0:T(2,128)(2,1)}, u32[]{:S(2)}, u32[]{:S(2)}) async-start(bf16[64,2,14336]{2,1,0:T(2,128)(2,1)} %reshape.16), calls=%async_computation.1 | async-start | bytes 7340032 | tf_op jit(solution)/shard_map/all_to_all | solution.py:73
  133.5 0.0 reduce-scatter.2.cloned.1.call-start
  133.5 2.1 collective-permute-start
  135.6 1.6 collective-permute-done
  137.2 2.6 convolution_multiply_fusion
  139.9 0.0 all-gather.5.cloned.1.call-start
  139.9 209.9 %all-to-all-done = bf16[64,2,14336]{2,1,0:T(2,128)(2,1)} async-done(((bf16[64,2,14336]{2,1,0:T(2,128)(2,1)}), bf16[64,2,14336]{2,1,0:T(2,128)(2,1)}, u32[]{:S(2)}, u32[]{:S(2)}) %all-to-all-start) | async-done | bytes 3670048 | tf_op jit(solution)/shard_map/all_to_all | solution.py:73
  349.9 19.3 %reshape.17 = bf16[2048,1,896]{2,1,0:T(2,128)(2,1)} reshape(bf16[64,2,14336]{2,1,0:T(2,128)(2,1)} %all-to-all-done) | data formatting | bytes 7340032
  369.2 3.7 copy.21
  372.9 0.5 convert_reduce_fusion
  373.5 0.2 copy-done.4
  373.7 0.0 copy-done.5
  373.7 0.7 fusion
  374.4 0.0 all-gather.3.cloned.1.call-start
  374.5 0.0 reduce-scatter.2.cloned.1.call-done
  374.6 1.1 multiply_reduce_fusion
  375.7 4.9 collective-permute-start.1
  380.6 1.9 collective-permute-start.2
  382.6 1.1 collective-permute-done.2
  383.7 1.8 multiply_convert_fusion.1
  385.5 0.0 all-gather.3.cloned.1.call-update
  385.5 110.6 %all-gather.5.cloned.1.call-done = bf16[896,2048]{0,1:T(8,128)(2,1)} async-done(((bf16[896,32]{0,1:T(8,128)(2,1)}), bf16[896,2048]{0,1:T(8,128)(2,1)}) %all-gather.5.cloned.1.call-update) | async-done | bytes 3670032 | tf_op jit(solution)/shard_map/all_gather | solution.py:81
  496.1 1.6 constant_dynamic-slice_fusion
  497.7 2.4 copy.23
  500.1 87.1 %all-gather.3.cloned.1.call-done = bf16[512,1024]{1,0:T(8,128)(2,1)} async-done(((bf16[64,1024]{1,0:T(8,128)(2,1)}), bf16[512,1024]{1,0:T(8,128)(2,1)}) %all-gather.3.cloned.1.call-update) | async-done | bytes 1048592 | tf_op jit(solution)/shard_map/all_gather | solution.py:64
  587.2 5.1 multiply_convert_fusion
  (20 shorter events, 0.1 us)
Async XLA Ops:
  17.8 4.9 copy-start
  117.0 16.5 %copy-start.7 = (bf16[256,896]{1,0:T(8,128)(2,1)S(1)}, bf16[256,896]{1,0:T(8,128)(2,1)}, u32[]{:S(2)}) copy-start(bf16[256,896]{1,0:T(8,128)(2,1)} %param.7) | copy-start | bytes 1376260
  117.0 20.2 %copy-start.1 = (bf16[896,1024]{1,0:T(8,128)(2,1)S(1)}, bf16[896,1024]{1,0:T(8,128)(2,1)}, u32[]{:S(2)}) copy-start(bf16[896,1024]{1,0:T(8,128)(2,1)} %param.11) | copy-start | bytes 5505028
  117.0 232.9 %all-to-all-start = ((bf16[64,2,14336]{2,1,0:T(2,128)(2,1)}), bf16[64,2,14336]{2,1,0:T(2,128)(2,1)}, u32[]{:S(2)}, u32[]{:S(2)}) async-start(bf16[64,2,14336]{2,1,0:T(2,128)(2,1)} %reshape.16), calls=%async_computation.1 | async-start | bytes 7340032 | tf_op jit(solution)/shard_map/all_to_all | solution.py:73
  133.5 241.1 %reduce-scatter.2.cloned.1.call-start = ((), (), s32[]{:S(2)}) async-start(), calls=%async_computation.2 | async-start | bytes 2359296 | tf_op jit(solution)/shard_map/reduce_scatter | solution.py:54
  133.5 3.7 collective-permute-start
  139.9 356.2 %all-gather.5.cloned.1.call-start = ((), (), s32[]{:S(2)}) async-start(), calls=%async_computation.4 | async-start | bytes 3727360 | tf_op jit(solution)/shard_map/all_gather | solution.py:81
  372.9 0.8 copy-start.4
  372.9 0.8 copy-start.5
  372.9 1.6 copy-start.6
  372.9 1.6 copy-start.2
  372.9 1.6 copy-start.3
  374.4 212.8 %all-gather.3.cloned.1.call-start = ((), (), s32[]{:S(2)}) async-start(), calls=%async_computation.3 | async-start | bytes 1179648 | tf_op jit(solution)/shard_map/all_gather | solution.py:64
  375.7 6.9 %collective-permute-start.1 = (f32[64]{0:T(128)S(1)}, f32[64]{0:T(128)S(1)}, u32[]{:S(2)}, u32[]{:S(2)}) collective-permute-start(f32[64]{0:T(128)S(1)} %get-tuple-element.10), channel_id=1, source_target_pairs={{0,8},{8,0},{16,24},{24,16},{32,40},{40,32},{48,56},{56,48},{64,72... | collective-permute-start | bytes 776 | tf_op jit(solution)/shard_map/ppermute | solution.py:16
  380.6 3.0 collective-permute-start.2
Sparse Core Ops, SparseCore 0:
  140.0 208.6 reduce-scatter.1
Sparse Core Ops, SparseCore 1:
  374.5 121.5 all-gather.4
  499.6 87.5 all-gather.2
where the time goes:
time: 601 us; the launch traced here: 600 us
  waiting for transfers between devices  410 us (68%)
  other arithmetic  84 us (14%)
  local copies, waits for them, and re-layouts  56.4 us (9%)
  starting transfers between devices  25.5 us (4%)
  between operations  15.7 us (3%)
  matrix products  7.78 us (1%)
    all_to_all x1, waiting for transfers between devices, local(): lax.all_to_all(buffer, 'replica', split_axis=2, concat_axis=0, tiled=True)  210 us
    all_gather x1, waiting for transfers between devices, local(): full_anchor = lax.all_gather(new_anchor, 'replica', axis=1, tiled=True)  111 us
    all_gather x1, waiting for transfers between devices, local(): lax.all_gather(slopes, 'tensor', axis=0, tiled=True)  87.1 us
    unnamed x1, other arithmetic  79.9 us
    unnamed x20, local copies, waits for them, and re-layouts  30.9 us
    all_to_all x1, starting transfers between devices, local(): lax.all_to_all(buffer, 'replica', split_axis=2, concat_axis=0, tiled=True)  16.5 us
  transfers between devices with their start and end apart: 7, of which 5 were waited for; matrix products, arithmetic and copies ran while one was open for 6% of the time, Pallas kernels for 0%

commit v1 on v0

--- a/solution.py
+++ b/solution.py
@@ -78,7 +78,9 @@
     new_anchor = (anchor_f - outer_rate * (pseudo + outer_mu * moment.astype(jnp.float32))).astype(
         jnp.bfloat16
     )
-    full_anchor = lax.all_gather(new_anchor, "replica", axis=1, tiled=True)
+    full_anchor = jnp.concatenate(
+        lax.all_to_all(jnp.stack([new_anchor] * lax.axis_size("replica")), "replica", 0, 0), axis=1
+    )
     own_anchor = lax.dynamic_slice_in_dim(full_anchor, side * half_cols, half_cols, 1)
     mixed = (mix_share * stepped + (1.0 - mix_share) * own_anchor.astype(jnp.float32)).astype(
         jnp.bfloat16

time: 601 us -> 661 us (1.100)
  blocking collectives: 0 us -> 179 us
  waiting for transfers between devices: 410 us -> 300 us
  starting transfers between devices: 25.5 us -> 16.1 us
    all_to_all x1, waiting for transfers between devices: 210 us -> 0.01 us  [local(): lax.all_to_all(jnp.stack([new_anchor] * lax.axis_size('replica')), 'repli...]
    reduce_scatter x1, waiting for transfers between devices: 0.02 us -> 208 us  [local(): lax.psum_scatter(jnp.dot(row_block, inner_weight, preferred_element_type=...]
    all_to_all x0 -> x1, blocking collectives: none -> 179 us  [local(): lax.all_to_all(buffer, 'replica', split_axis=2, concat_axis=0, tiled=True)]
    all_gather x1 -> x0, waiting for transfers between devices: 111 us -> none  [local(): full_anchor = lax.all_gather(new_anchor, 'replica', axis=1, tiled=True)]
    all_to_all x1, starting transfers between devices: 16.5 us -> 9.67 us  [local(): lax.all_to_all(jnp.stack([new_anchor] * lax.axis_size('replica')), 'repli...]
  transfers between devices with their start and end apart: 7 -> 6, of which waited for: 5 -> 4; matrix products, arithmetic and copies ran while one was open for 6% -> 1% of each run, Pallas kernels for 0% -> 0%
where the time goes in v1:
time: 661 us; the launch traced here: 660 us
  waiting for transfers between devices  300 us (45%)
  blocking collectives  179 us (27%)
  other arithmetic  84 us (13%)
  local copies, waits for them, and re-layouts  59.1 us (9%)
  starting transfers between devices  16.1 us (2%)
  between operations  14.2 us (2%)
  matrix products  7.78 us (1%)
    reduce_scatter x1, waiting for transfers between devices, local(): lax.psum_scatter(jnp.dot(row_block, inner_weight, preferred_element_type=...  208 us
    all_to_all x1, blocking collectives, local(): lax.all_to_all(buffer, 'replica', split_axis=2, concat_axis=0, tiled=True)  179 us
    all_gather x1, waiting for transfers between devices, local(): lax.all_gather(slopes, 'tensor', axis=0, tiled=True)  89.2 us
    unnamed x1, other arithmetic  79.8 us
    unnamed x20, local copies, waits for them, and re-layouts  31.5 us
  transfers between devices with their start and end apart: 6, of which 4 were waited for; matrix products, arithmetic and copies ran while one was open for 1% of the time, Pallas kernels for 0%

profile of v1, /device:TPU:8, one launch (start us, length us, event | category | flops | bytes accessed | tf_op | source)
XLA Modules:
  0.0 659.6 jit_solution(17404095857106054309)
XLA Ops:
  7.2 9.7 %copy.16 = bf16[1,896,1024]{1,0,2:T(2,128)(2,1)} copy(bf16[1,896,1024]{2,1,0:T(8,128)(2,1)} %bitcast.12) | data formatting | bytes 3670016 | tf_op jit(solution)/shard_map/broadcast_in_dim | solution.py:72
  16.9 4.9 broadcast_in_dim.4
  21.8 5.6 constant_dynamic-update-slice_fusion
  27.4 0.5 broadcast.29
  27.9 79.8 %reduce.3 = bf16[2048,896]{1,0:T(8,128)(2,1)} reduce(bf16[2048,1,896]{2,1,0:T(2,128)(2,1)} %bitcast.6, bf16[]{:T(256)} %broadcast.29), dimensions={1}, to_apply=%bitcast.6.reduce_sub_computation | reduce | bytes 7340034
  107.7 8.3 %reshape.26 = bf16[64,2,14336]{2,1,0:T(2,128)(2,1)} reshape(bf16[2048,896]{1,0:T(8,128)(2,1)} %reduce.3) | data formatting | bytes 7340032
  116.0 178.7 %all_to_all.14 = bf16[64,2,14336]{2,1,0:T(2,128)(2,1)} all-to-all(bf16[64,2,14336]{2,1,0:T(2,128)(2,1)} %reshape.26), channel_id=1, replica_groups=mesh['replica'=64,'tensor'=8] {'replica'}, dimensions={0} | all-to-all | bytes 7340032 | tf_op jit(solution)/shard_map/all_to_all | solution.py:73
  294.7 19.3 %reshape.27 = bf16[2048,1,896]{2,1,0:T(2,128)(2,1)} reshape(bf16[64,2,14336]{2,1,0:T(2,128)(2,1)} %all_to_all.14) | data formatting | bytes 7340032
  314.0 3.7 copy.17
  317.7 0.5 convert_reduce_fusion
  318.3 0.3 copy-done.4
  318.5 0.0 copy-done.5
  318.6 0.7 fusion
  319.2 2.1 stack.2
  321.3 9.7 %all-to-all-start.1 = ((bf16[64,896,32]{1,2,0:T(8,128)(2,1)}), bf16[64,896,32]{1,2,0:T(8,128)(2,1)}, u32[]{:S(2)}, u32[]{:S(2)}) async-start(bf16[64,896,32]{1,2,0:T(8,128)(2,1)} %stack.2), calls=%async_computation.2 | async-start | bytes 7340032 | tf_op jit(solution)/shard_map/all_to_all | solution.py:82
  331.0 0.0 reduce-scatter.2.cloned.1.call-start
  331.1 2.1 collective-permute-start
  333.1 1.6 collective-permute-done
  334.8 2.6 convolution_multiply_fusion
  337.5 0.0 all-gather.2.cloned.1.call-start
  337.5 0.6 copy-done.6
  338.1 208.1 %reduce-scatter.2.cloned.1.call-done = f32[64,1024]{1,0:T(8,128)} async-done(((f32[512,1024]{1,0:T(8,128)}), f32[64,1024]{1,0:T(8,128)}) %reduce-scatter.2.cloned.1.call-update) | async-done | bytes 262160 | tf_op jit(solution)/shard_map/reduce_scatter | solution.py:54
  546.2 1.1 multiply_reduce_fusion
  547.4 1.9 collective-permute-start.1
  549.3 2.4 collective-permute-start.2
  551.7 0.8 collective-permute-done.2
  552.5 1.8 multiply_convert_fusion.1
  554.3 0.0 all-gather.2.cloned.1.call-update
  554.3 1.7 constant_dynamic-slice_fusion
  556.0 2.4 copy.19
  558.4 89.2 %all-gather.2.cloned.1.call-done = bf16[512,1024]{1,0:T(8,128)(2,1)} async-done(((bf16[64,1024]{1,0:T(8,128)(2,1)}), bf16[512,1024]{1,0:T(8,128)(2,1)}) %all-gather.2.cloned.1.call-update) | async-done | bytes 1048592 | tf_op jit(solution)/shard_map/all_gather | solution.py:64
  647.6 5.1 multiply_convert_fusion
  (19 shorter events, 0.1 us)
Async XLA Ops:
  16.9 4.9 copy-start
  317.7 0.8 copy-start.4
  317.7 0.8 copy-start.5
  321.3 9.7 %copy-start.7 = (bf16[256,896]{1,0:T(8,128)(2,1)S(1)}, bf16[256,896]{1,0:T(8,128)(2,1)}, u32[]{:S(2)}) copy-start(bf16[256,896]{1,0:T(8,128)(2,1)} %param.7) | copy-start | bytes 1376260
  321.3 13.4 %copy-start.1 = (bf16[896,1024]{1,0:T(8,128)(2,1)S(1)}, bf16[896,1024]{1,0:T(8,128)(2,1)}, u32[]{:S(2)}) copy-start(bf16[896,1024]{1,0:T(8,128)(2,1)} %param.11) | copy-start | bytes 5505028
  321.3 233.0 %all-to-all-start.1 = ((bf16[64,896,32]{1,2,0:T(8,128)(2,1)}), bf16[64,896,32]{1,2,0:T(8,128)(2,1)}, u32[]{:S(2)}, u32[]{:S(2)}) async-start(bf16[64,896,32]{1,2,0:T(8,128)(2,1)} %stack.2), calls=%async_computation.2 | async-start | bytes 7340032 | tf_op jit(solution)/shard_map/all_to_all | solution.py:82
  331.0 215.2 %reduce-scatter.2.cloned.1.call-start = ((), (), s32[]{:S(2)}) async-start(), calls=%async_computation.3 | async-start | bytes 2359296 | tf_op jit(solution)/shard_map/reduce_scatter | solution.py:54
  331.1 3.7 collective-permute-start
  337.4 0.7 copy-start.6
  337.4 208.8 %copy-start.2 = (bf16[64,1024]{1,0:T(8,128)(2,1)S(1)}, bf16[64,1024]{1,0:T(8,128)(2,1)}, u32[]{:S(2)}) copy-start(bf16[64,1024]{1,0:T(8,128)(2,1)} %param.9) | copy-start | bytes 393220
  337.4 208.8 %copy-start.3 = (bf16[64,1024]{1,0:T(8,128)(2,1)S(1)}, bf16[64,1024]{1,0:T(8,128)(2,1)}, u32[]{:S(2)}) copy-start(bf16[64,1024]{1,0:T(8,128)(2,1)} %param.8) | copy-start | bytes 393220
  337.5 310.1 %all-gather.2.cloned.1.call-start = ((), (), s32[]{:S(2)}) async-start(), calls=%async_computation.4 | async-start | bytes 1179648 | tf_op jit(solution)/shard_map/all_gather | solution.py:64
  547.4 4.3 collective-permute-start.1
  549.3 3.2 collective-permute-start.2
Sparse Core Ops, SparseCore 0:
  337.6 208.5 reduce-scatter.1
  554.4 93.1 all-gather.1

commit v2 on v0

--- a/solution.py
+++ b/solution.py
@@ -70,7 +70,12 @@
     replica_count = lax.axis_size("replica") // 2
     buffer = jnp.zeros((1, ff_local, total_features), jnp.bfloat16)
     buffer = lax.dynamic_update_slice(buffer, inner_weight[None], (0, 0, side * half_cols))
-    received = lax.all_to_all(buffer, "replica", split_axis=2, concat_axis=0, tiled=True)
+    received = jnp.concatenate(
+        lax.all_to_all(
+            jnp.stack(jnp.split(buffer, lax.axis_size("replica"), axis=2)), "replica", 0, 0
+        ),
+        axis=0,
+    )
     summed = jnp.sum(received, axis=0, dtype=jnp.float32)
     anchor_f = anchor.astype(jnp.float32)
     pseudo = anchor_f - summed / replica_count

time: 601 us -> 514 us (0.86)
  other arithmetic: 84 us -> 6.22 us
  local copies, waits for them, and re-layouts: 56.4 us -> 47.7 us
    unnamed x1 -> x0, other arithmetic: 79.9 us -> none
    unnamed x20 -> x79, local copies, waits for them, and re-layouts: 30.9 us -> 44.9 us
    broadcast_in_dim x1 -> x0, local copies, waits for them, and re-layouts: 9.79 us -> none  [local(): inner_weight[None]]
  transfers between devices with their start and end apart: 7 -> 7, of which waited for: 5 -> 5; matrix products, arithmetic and copies ran while one was open for 6% -> 3% of each run, Pallas kernels for 0% -> 0%
where the time goes in v2:
time: 514 us; the launch traced here: 513 us
  waiting for transfers between devices  410 us (80%)
  local copies, waits for them, and re-layouts  47.7 us (9%)
  starting transfers between devices  25.5 us (5%)
  between operations  15.7 us (3%)
  matrix products  7.79 us (2%)
  other arithmetic  6.22 us (1%)
    all_to_all x1, waiting for transfers between devices, local(): lax.all_to_all(jnp.stack(jnp.split(buffer, lax.axis_size('replica'), axis...  210 us
    all_gather x1, waiting for transfers between devices, local(): full_anchor = lax.all_gather(new_anchor, 'replica', axis=1, tiled=True)  111 us
    all_gather x1, waiting for transfers between devices, local(): lax.all_gather(slopes, 'tensor', axis=0, tiled=True)  87.1 us
    unnamed x79, local copies, waits for them, and re-layouts  44.9 us
    all_to_all x1, starting transfers between devices, local(): lax.all_to_all(jnp.stack(jnp.split(buffer, lax.axis_size('replica'), axis...  16.5 us
  transfers between devices with their start and end apart: 7, of which 5 were waited for; matrix products, arithmetic and copies ran while one was open for 3% of the time, Pallas kernels for 0%

profile of v2, /device:TPU:8, one launch (start us, length us, event | category | flops | bytes accessed | tf_op | source)
XLA Modules:
  0.0 513.3 jit_solution(14849957771674007304)
XLA Ops:
  8.0 3.1 copy.13
  13.5 0.6 constant_dynamic-update-slice_fusion.60
  14.2 0.6 constant_dynamic-update-slice_fusion.59
  15.4 0.6 constant_dynamic-update-slice_fusion.57
  18.5 0.6 constant_dynamic-update-slice_fusion.52
  19.2 0.6 constant_dynamic-update-slice_fusion.51
  21.1 0.6 constant_dynamic-update-slice_fusion.48
  21.7 0.6 constant_dynamic-update-slice_fusion.47
  24.2 0.6 constant_dynamic-update-slice_fusion.43
  26.7 0.6 constant_dynamic-update-slice_fusion.39
  29.8 0.6 constant_dynamic-update-slice_fusion.34
  30.5 0.6 constant_dynamic-update-slice_fusion.33
  33.6 0.6 constant_dynamic-update-slice_fusion.28
  36.1 0.6 constant_dynamic-update-slice_fusion.24
  44.2 0.6 constant_dynamic-update-slice_fusion.11
  51.7 16.5 %all-to-all-start = ((bf16[64,1,896,32]{2,3,1,0:T(8,128)(2,1)}), bf16[64,1,896,32]{2,3,1,0:T(8,128)(2,1)}, u32[]{:S(2)}, u32[]{:S(2)}) async-start(bf16[64,1,896,32]{2,3,1,0:T(8,128)(2,1)} %constant_dynamic-update-slice_fusion), calls=%async_computation.1 | async-start | bytes 7340032 | tf_op jit(solution)/shard_map/all_to_all | solution.py:74
  68.3 2.1 collective-permute-start
  70.3 1.6 collective-permute-done
  72.0 2.7 convolution_multiply_fusion
  74.7 209.9 %all-to-all-done = bf16[64,1,896,32]{2,3,1,0:T(8,128)(2,1)} async-done(((bf16[64,1,896,32]{2,3,1,0:T(8,128)(2,1)}), bf16[64,1,896,32]{2,3,1,0:T(8,128)(2,1)}, u32[]{:S(2)}, u32[]{:S(2)}) %all-to-all-start) | async-done | bytes 3670048 | tf_op jit(solution)/shard_map/all_to_all | solution.py:74
  284.7 2.6 convert_reduce_fusion
  287.2 0.7 fusion
  288.1 1.1 multiply_reduce_fusion
  289.2 4.9 collective-permute-start.1
  294.2 1.9 collective-permute-start.2
  296.1 1.1 collective-permute-done.2
  297.2 1.8 multiply_convert_fusion.1
  299.0 110.6 %all-gather.5.cloned.1.call-done = bf16[896,2048]{0,1:T(8,128)(2,1)} async-done(((bf16[896,32]{0,1:T(8,128)(2,1)}), bf16[896,2048]{0,1:T(8,128)(2,1)}) %all-gather.5.cloned.1.call-update) | async-done | bytes 3670032 | tf_op jit(solution)/shard_map/all_gather | solution.py:86
  409.6 1.6 constant_dynamic-slice_fusion
  411.2 2.4 copy.15
  413.6 87.1 %all-gather.3.cloned.1.call-done = bf16[512,1024]{1,0:T(8,128)(2,1)} async-done(((bf16[64,1024]{1,0:T(8,128)(2,1)}), bf16[512,1024]{1,0:T(8,128)(2,1)}) %all-gather.3.cloned.1.call-update) | async-done | bytes 1048592 | tf_op jit(solution)/shard_map/all_gather | solution.py:64
  500.7 5.1 %multiply_convert_fusion = bf16[896,1024]{1,0:T(8,128)(2,1)} fusion(bf16[896,1024]{1,0:T(8,128)(2,1)} %copy.15, bf16[896,1024]{1,0:T(8,128)(2,1)} %param.11, bf16[512,1024]{1,0:T(8,128)(2,1)} %all-gather.3.cloned.1.call-done, bf16[256,896]{1,0:T(8,128)(2,1)S(1)} %collective-permute-done, bf16[256,896]{1,0:T(8,128)(2,1)S(1)} %copy-done.6, pred[]{:T(512)S(6)} %eq.5), kind=kOutput, calls=%fused_computation.1 | convolution fusion | flops 950075392 | bytes 7471105 | tf_op jit(solution)/shard_map/dot_general | solution.py:62
  (77 shorter events, 32.0 us)
Async XLA Ops:
  51.7 16.5 %copy-start.6 = (bf16[256,896]{1,0:T(8,128)(2,1)S(1)}, bf16[256,896]{1,0:T(8,128)(2,1)}, u32[]{:S(2)}) copy-start(bf16[256,896]{1,0:T(8,128)(2,1)} %param.7) | copy-start | bytes 1376260
  51.7 20.2 %copy-start = (bf16[896,1024]{1,0:T(8,128)(2,1)S(1)}, bf16[896,1024]{1,0:T(8,128)(2,1)}, u32[]{:S(2)}) copy-start(bf16[896,1024]{1,0:T(8,128)(2,1)} %param.11) | copy-start | bytes 5505028
  51.7 232.9 %all-to-all-start = ((bf16[64,1,896,32]{2,3,1,0:T(8,128)(2,1)}), bf16[64,1,896,32]{2,3,1,0:T(8,128)(2,1)}, u32[]{:S(2)}, u32[]{:S(2)}) async-start(bf16[64,1,896,32]{2,3,1,0:T(8,128)(2,1)} %constant_dynamic-update-slice_fusion), calls=%async_computation.1 | async-start | bytes 7340032 | tf_op jit(solution)/shard_map/all_to_all | solution.py:74
  68.2 219.8 %reduce-scatter.2.cloned.1.call-start = ((), (), s32[]{:S(2)}) async-start(), calls=%async_computation.2 | async-start | bytes 2359296 | tf_op jit(solution)/shard_map/reduce_scatter | solution.py:54
  68.3 3.7 collective-permute-start
  74.6 212.6 %copy-start.3 = (bf16[896,32]{0,1:T(8,128)(2,1)S(1)}, bf16[896,32]{0,1:T(8,128)(2,1)}, u32[]{:S(2)}) copy-start(bf16[896,32]{0,1:T(8,128)(2,1)} %param.12) | copy-start | bytes 172036
  74.6 212.6 %copy-start.4 = (bf16[896,32]{0,1:T(8,128)(2,1)S(1)}, bf16[896,32]{0,1:T(8,128)(2,1)}, u32[]{:S(2)}) copy-start(bf16[896,32]{0,1:T(8,128)(2,1)} %param.13) | copy-start | bytes 172036
  74.7 213.4 %copy-start.5 = (bf16[2048]{0:T(1024)(128)(2,1)S(1)}, bf16[2048]{0:T(1024)(128)(2,1)}, u32[]{:S(2)}) copy-start(bf16[2048]{0:T(1024)(128)(2,1)} %param.10) | copy-start | bytes 12292
  74.7 213.4 %copy-start.1 = (bf16[64,1024]{1,0:T(8,128)(2,1)S(1)}, bf16[64,1024]{1,0:T(8,128)(2,1)}, u32[]{:S(2)}) copy-start(bf16[64,1024]{1,0:T(8,128)(2,1)} %param.9) | copy-start | bytes 393220
  74.7 213.4 %copy-start.2 = (bf16[64,1024]{1,0:T(8,128)(2,1)S(1)}, bf16[64,1024]{1,0:T(8,128)(2,1)}, u32[]{:S(2)}) copy-start(bf16[64,1024]{1,0:T(8,128)(2,1)} %param.8) | copy-start | bytes 393220
  74.7 334.9 %all-gather.5.cloned.1.call-start = ((), (), s32[]{:S(2)}) async-start(), calls=%async_computation.4 | async-start | bytes 3727360 | tf_op jit(solution)/shard_map/all_gather | solution.py:86
  288.0 212.8 %all-gather.3.cloned.1.call-start = ((), (), s32[]{:S(2)}) async-start(), calls=%async_computation.3 | async-start | bytes 1179648 | tf_op jit(solution)/shard_map/all_gather | solution.py:64
  289.2 6.9 %collective-permute-start.1 = (f32[64]{0:T(128)S(1)}, f32[64]{0:T(128)S(1)}, u32[]{:S(2)}, u32[]{:S(2)}) collective-permute-start(f32[64]{0:T(128)S(1)} %get-tuple-element.7), channel_id=1, source_target_pairs={{0,8},{8,0},{16,24},{24,16},{32,40},{40,32},{48,56},{56,48},{64,72... | collective-permute-start | bytes 776 | tf_op jit(solution)/shard_map/ppermute | solution.py:16
  294.2 3.0 collective-permute-start.2
Sparse Core Ops, SparseCore 0:
  74.8 208.5 reduce-scatter.1
Sparse Core Ops, SparseCore 1:
  288.0 121.5 all-gather.4
  413.2 87.5 all-gather.2
